TPU v7x, 32 devices: a whole 2x2x4 slice. The times are simulated.
32 devices in a mesh: mp: 2 (over core), feat: 16 (over z, y, x).
Axes of the slice: x: 2, y: 2, z: 4, core: 2. Of those that a mesh axis runs over, the one named last changes fastest.
Arguments:
- residual: bfloat16 [2, 96, 2304], P(None, 'feat', 'mp'), may hold values from -6 to 6
- norm_gain: float32 [2, 2304], P(None, 'mp'), may hold values from 0.1 to 1.9
- gate_weight: bfloat16 [2, 2304, 9216], P(None, 'mp', 'feat'), may hold values from -0.125 to 0.125
- up_weight: bfloat16 [2, 2304, 9216], P(None, 'mp', 'feat'), may hold values from -0.125 to 0.125
- down_weight: bfloat16 [2, 9216, 2304], P(None, 'feat', 'mp'), may hold values from -0.0625 to 0.0625
- encoder: bfloat16 [2, 32768, 2304], P(None, 'feat', 'mp'), may hold values from -0.125 to 0.125
- encoder_bias: float32 [2, 32768], P(None, 'feat'), may hold values from -3 to 3
- decoder: bfloat16 [3, 32768, 2304], P(None, 'feat', 'mp'), may hold values from -0.03125 to 0.03125
Outputs:
- grad_encoder: bfloat16 [2, 32768, 2304], P(None, 'feat', 'mp')
- grad_bias: float32 [2, 32768], P(None, 'feat')
- grad_decoder: bfloat16 [3, 32768, 2304], P(None, 'feat', 'mp')
All inputs are finite; a program needn't handle non-finite values.
Results may differ from a plain program's by a relative error of at most 0.02.
The roundings to bfloat16 on the way count: a program that leaves them out, or rounds other values in their place, can miss the bound.
Values may be sent and summed in bfloat16 or wider, within the bound.
No kernel may reach another device: no remote copies, remote signals or barrier semaphores. Data moves between devices by JAX's collectives and lax.ppermute only.
A program may use at most 128 MiB of HBM per device.

v0:
```python
import math
import jax
import jax.numpy as jnp
from jax import lax
from jax.sharding import PartitionSpec as P

D = 2304
sparsity_weight = 0.1


def outer_product(weights_side, errors_side):
    return lax.dot_general(
        weights_side, errors_side, (((0,), (0,)), ((), ())), preferred_element_type=jnp.float32
    )


def body(residual, norm_gain, gate_weight, up_weight, down_weight, encoder, encoder_bias, decoder):
    values = residual.astype(jnp.float32)
    squares = lax.psum(jnp.sum(values * values, axis=2), "mp")
    inverse_rms = lax.rsqrt(squares / D + 1e-06)
    normed_local = (values * inverse_rms[:, :, None] * norm_gain[:, None, :]).astype(jnp.bfloat16)
    normed = lax.all_gather(normed_local, "feat", axis=1, tiled=True)
    tokens = normed.shape[1]
    local_rows = residual.shape[1]
    gate_part = jnp.einsum("ltd,ldh->lth", normed, gate_weight, preferred_element_type=jnp.float32)
    up_part = jnp.einsum("ltd,ldh->lth", normed, up_weight, preferred_element_type=jnp.float32)
    gate_part, up_part = (
        lax.psum(gate_part.astype(jnp.bfloat16), "mp").astype(jnp.float32),
        lax.psum(up_part.astype(jnp.bfloat16), "mp").astype(jnp.float32),
    )
    hidden = (jax.nn.gelu(gate_part, approximate=True) * up_part).astype(jnp.bfloat16)
    preact_part = jnp.einsum("ltd,lfd->tlf", normed, encoder, preferred_element_type=jnp.float32)
    preact = lax.psum(preact_part, "mp")
    active = jnp.maximum(preact + encoder_bias[None], 0.0).astype(jnp.bfloat16)
    features = active.shape[2]
    model_cols = decoder.shape[2]
    joined = jnp.concatenate([decoder[1], decoder[2]], axis=0)
    picked = hidden
    partial_value = jnp.einsum(
        "lth,lhd->tld", picked, down_weight, preferred_element_type=jnp.float32
    )
    picked = active
    first_part = jnp.dot(picked[:, 0], decoder[0], preferred_element_type=jnp.float32)
    second = jnp.dot(
        picked.reshape(local_rows * lax.axis_size("feat"), 2 * features),
        joined,
        preferred_element_type=jnp.float32,
    )
    errors_local = lax.psum_scatter(
        jnp.concatenate([first_part, second], axis=1)
        - partial_value.reshape(local_rows * lax.axis_size("feat"), -1),
        "feat",
        scatter_dimension=0,
        tiled=True,
    ).astype(jnp.bfloat16)
    errors = lax.all_gather(errors_local, "feat", axis=0, tiled=True)
    error_first = errors[:, :model_cols]
    error_second = errors[:, model_cols:]
    first_rows = jnp.concatenate([decoder[0], decoder[1]], axis=1)
    back_first = lax.dot_general(
        errors, first_rows, (((1,), (1,)), ((), ())), preferred_element_type=jnp.float32
    )
    back_second = lax.dot_general(
        error_second, decoder[2], (((1,), (1,)), ((), ())), preferred_element_type=jnp.float32
    )
    back_stack = jnp.stack([back_first, back_second], axis=1)
    loss_scale = 1.0 / math.sqrt(tokens)
    backward = lax.psum(back_stack.astype(jnp.bfloat16), "mp").astype(jnp.float32)
    pre_grad = jnp.where(active > 0, loss_scale * (backward + sparsity_weight), 0.0).astype(
        jnp.bfloat16
    )
    grad_encoder = jnp.einsum(
        "tlf,ltd->lfd", pre_grad, normed, preferred_element_type=jnp.float32
    ).astype(jnp.bfloat16)
    grad_bias = jnp.sum(pre_grad.astype(jnp.float32), axis=0)
    active_first = active[:, 0]
    active_second = active[:, 1]
    grad_decoder = (
        loss_scale
        * jnp.stack(
            [
                outer_product(active_first, error_first),
                outer_product(active_first, error_second),
                outer_product(active_second, error_second),
            ]
        )
    ).astype(jnp.bfloat16)
    return (grad_encoder, grad_bias, grad_decoder)


def solution(mesh):
    return jax.shard_map(
        body,
        mesh=mesh,
        in_specs=(
            P(None, "feat", "mp"),
            P(None, "mp"),
            P(None, "mp", "feat"),
            P(None, "mp", "feat"),
            P(None, "feat", "mp"),
            P(None, "feat", "mp"),
            P(None, "feat"),
            P(None, "feat", "mp"),
        ),
        out_specs=(P(None, "feat", "mp"), P(None, "feat"), P(None, "feat", "mp")),
        check_vma=False,
    )
```

profile of v0, /device:TPU:0, one launch (start us, length us, event | category | flops | bytes accessed | tf_op | source)
XLA Modules:
  0.0 270.2 jit_solution(11253927287694514613)
XLA Ops:
  8.2 2.6 psum.35
  11.7 44.8 %all_gather.6 = bf16[2,96,1152]{2,0,1:T(2,128)(2,1)S(1)} all-gather(bf16[2,6,1152]{2,0,1:T(2,128)(2,1)S(1)} %fusion.40), channel_id=1, replica_groups=mesh['mp'=2,'feat'=16] {'feat'}, dimensions={1}, use_global_device_ids=true | all-gather | bytes 470016 | tf_op jit(solution)/shard_map/all_gather | solution.py:22
  56.5 3.6 %convolution_convert_fusion.3 = bf16[2,96,576]{2,1,0:T(8,128)(2,1)} fusion(bf16[2,1152,576]{1,2,0:T(8,128)(2,1)} %param.10, bf16[2,96,1152]{2,0,1:T(2,128)(2,1)S(1)} %all_gather.6), kind=kOutput, calls=%fused_computation.27 | convolution fusion | flops 254914560 | bytes 3317760 | tf_op jit(solution)/shard_map/ltd,ldh->lth/dot_general | solution.py:25
  60.1 3.4 %convolution_convert_fusion.2 = bf16[2,96,576]{2,1,0:T(8,128)(2,1)} fusion(bf16[2,1152,576]{1,2,0:T(8,128)(2,1)} %param.11, bf16[2,96,1152]{2,0,1:T(2,128)(2,1)S(1)} %all_gather.6), kind=kOutput, calls=%fused_computation.26 | convolution fusion | flops 254914560 | bytes 3317760 | tf_op jit(solution)/shard_map/ltd,ldh->lth/dot_general | solution.py:26
  63.6 8.0 %convolution_bitcast_fusion.4 = f32[96,2,2048]{2,0,1:T(8,128)} fusion(bf16[2,2048,1152]{2,1,0:T(8,128)(2,1)} %param.13, bf16[2,96,1152]{2,0,1:T(2,128)(2,1)S(1)} %all_gather.6), kind=kOutput, calls=%fused_computation.18 | convolution fusion | flops 905969664 | bytes 11452416 | tf_op jit(solution)/shard_map/ltd,lfd->tlf/dot_general | solution.py:32
  71.7 11.3 %slice_bitcast_fusion.2 = (bf16[2048,1152]{1,0:T(8,128)(2,1)}, bf16[2048,1152]{1,0:T(8,128)(2,1)}, bf16[2048,1152]{1,0:T(8,128)(2,1)}) fusion(bf16[3,2048,1152]{2,1,0:T(8,128)(2,1)} %param.15), kind=kLoop, calls=%fused_computation.16 | loop fusion | bytes 28311552 | tf_op jit(solution)/shard_map/squeeze | solution.py:43
  83.0 1.7 convolution_bitcast_fusion.3
  84.8 17.4 %all-reduce.7.cloned.1.call-done = f32[96,2,2048]{2,0,1:T(8,128)} async-done(((f32[96,2,2048]{2,0,1:T(8,128)}), f32[96,2,2048]{2,0,1:T(8,128)}) %all-reduce.7.cloned.1.call-update) | async-done | bytes 1572880 | tf_op jit(solution)/shard_map/psum | solution.py:33
  102.1 1.7 maximum_convert_fusion
  103.9 3.7 %fusion.24 = f32[96,1152]{1,0:T(8,128)S(1)} fusion(bf16[96,2,2048]{2,0,1:T(8,128)(2,1)S(1)} %maximum_convert_fusion, bf16[3,2048,1152]{2,1,0:T(8,128)(2,1)} %param.15), kind=kOutput, calls=%fused_computation.43 | convolution fusion | flops 452984832 | bytes 5554176 | tf_op jit(solution)/shard_map/dot_general | solution.py:43
  108.5 2.0 fusion.2
  110.6 49.0 %fusion = f32[8,2304]{1,0:T(8,128)S(1)} fusion(f32[96,2304]{1,0:T(8,128)S(1)} %maximum_subtract_fusion), kind=kCustom, calls=%all-reduce-scatter | all-reduce-scatter fusion | flops 294913 | bytes 958976
  159.6 1.3 collective-permute-start.1
  162.2 1.9 collective-permute-start
  164.1 2.4 collective-permute-start.3
  168.8 43.6 %all-gather = bf16[16,6,2304]{2,1,0:T(8,128)(2,1)S(1)} all-gather(bf16[1,6,2304]{2,1,0:T(8,128)(2,1)S(1)} %fusion.41), channel_id=1, replica_groups=mesh['mp'=2,'feat'=16] {'feat'}, dimensions={0}, use_global_device_ids=true | all-gather | bytes 470016 | tf_op jit(solution)/shard_map/all_gather | solution.py:56
  212.5 3.9 %fusion.16 = bf16[96,1,2048]{2,0,1:T(8,128)(2,1)S(1)} fusion(bf16[96,2304]{1,0:T(8,128)(2,1)S(1)} %reshape.18, bf16[3,2048,1152]{2,1,0:T(8,128)(2,1)} %param.15), kind=kOutput, calls=%fused_computation.22 | convolution fusion | flops 453181440 | bytes 5332992 | tf_op jit(solution)/shard_map/dot_general | solution.py:63
  216.4 5.1 %convolution_bitcast_fusion.1 = f32[1,2048,1152]{2,1,0:T(8,128)} fusion(bf16[96,2,2048]{2,0,1:T(8,128)(2,1)S(1)} %maximum_convert_fusion, bf16[96,2304]{1,0:T(8,128)(2,1)S(1)} %reshape.18), kind=kOutput, calls=%fused_computation.12 | convolution fusion | flops 452984832 | bytes 10051584 | tf_op jit(solution)/shard_map/dot_general | solution.py:12
  221.5 5.8 %convolution_bitcast_fusion = f32[1,2048,1152]{2,1,0:T(8,128)} fusion(bf16[96,2,2048]{2,0,1:T(8,128)(2,1)S(1)} %maximum_convert_fusion, bf16[96,2304]{1,0:T(8,128)(2,1)S(1)} %reshape.18), kind=kOutput, calls=%fused_computation.11 | convolution fusion | flops 452984832 | bytes 10051584 | tf_op jit(solution)/shard_map/dot_general | solution.py:12
  227.3 5.1 %convolution_bitcast_fusion.2 = f32[1,2048,1152]{2,1,0:T(8,128)} fusion(bf16[96,2,2048]{2,0,1:T(8,128)(2,1)S(1)} %maximum_convert_fusion, bf16[96,2304]{1,0:T(8,128)(2,1)S(1)} %reshape.18), kind=kOutput, calls=%fused_computation.13 | convolution fusion | flops 452984832 | bytes 10051584 | tf_op jit(solution)/shard_map/dot_general | solution.py:12
  232.4 3.1 %fusion.13 = bf16[96,1,2048]{2,0,1:T(8,128)(2,1)S(1)} fusion(bf16[96,2304]{1,0:T(8,128)(2,1)S(1)} %reshape.18, bf16[2048,1152]{1,0:T(8,128)(2,1)S(1)} %bitcast.51, bf16[2048,1152]{1,0:T(8,128)(2,1)S(1)} %bitcast.47), kind=kOutput, calls=%fused_computation.21 | convolution fusion | flops 925040640 | bytes 10272768 | tf_op jit(solution)/shard_map/dot_general | solution.py:60
  236.5 16.6 %fusion.1 = bf16[3,2048,1152]{2,1,0:T(8,128)(2,1)} fusion(f32[1,2048,1152]{2,1,0:T(8,128)} %convolution_bitcast_fusion, f32[1,2048,1152]{2,1,0:T(8,128)} %convolution_bitcast_fusion.1, f32[1,2048,1152]{2,1,0:T(8,128)} %convolution_bitcast_fusion.2), kind=kLoop, calls=%fused_computation.1 | loop fusion | flops 28311552 | bytes 42467328 | tf_op jit(solution)/shard_map/convert_element_type | solution.py:87
  253.2 2.8 %convert_reduce_fusion = f32[2,2048]{1,0:T(2,128)} fusion(bf16[96,2,2048]{2,0,1:T(8,128)(2,1)} %all-reduce.9.cloned.1.call-done, f32[96,2,2048]{2,0,1:T(8,128)} %all-reduce.7.cloned.1.call-done, f32[2,2048]{1,0:T(2,128)S(1)} %copy-done.5), kind=kLoop, calls=%fused_computation.23 | loop fusion | flops 4321280 | bytes 2392064 | tf_op jit(solution)/shard_map/reduce_sum | solution.py:75
  256.0 7.6 %convolution_convert_fusion = bf16[2,2048,1152]{2,1,0:T(8,128)(2,1)} fusion(bf16[2,96,1152]{2,0,1:T(2,128)(2,1)} %copy-done.3, bf16[96,2,2048]{2,0,1:T(8,128)(2,1)} %all-reduce.9.cloned.1.call-done, bf16[96,2,2048]{2,0,1:T(8,128)(2,1)S(1)} %maximum_convert_fusion), kind=kOutput, calls=%fused_computation.2 | convolution fusion | flops 913047552 | bytes 11452416 | tf_op jit(solution)/shard_map/tlf,ltd->lfd/dot_general | solution.py:72
  (56 shorter events, 7.1 us)
Async XLA Ops:
  7.2 75.8 %copy-start = (bf16[2,576,1152]{2,1,0:T(8,128)(2,1)S(1)}, bf16[2,576,1152]{2,1,0:T(8,128)(2,1)}, u32[]{:S(2)}) copy-start(bf16[2,576,1152]{2,1,0:T(8,128)(2,1)} %param.12) | copy-start | bytes 7962628
  7.2 75.8 %all-reduce.11.cloned.1.call-start = ((), (), s32[]{:S(2)}) async-start(), calls=%async_computation.2 | async-start | bytes 983040 | tf_op jit(solution)/shard_map/psum | solution.py:28
  56.5 15.0 %copy-start.3 = (bf16[2,96,1152]{2,0,1:T(2,128)(2,1)}, bf16[2,96,1152]{2,0,1:T(2,128)(2,1)S(1)}, u32[]{:S(2)}) copy-start(bf16[2,96,1152]{2,0,1:T(2,128)(2,1)S(1)} %all_gather.6) | copy-start | bytes 1327108
  63.5 38.6 %all-reduce.7.cloned.1.call-start = ((), (), s32[]{:S(2)}) async-start(), calls=%async_computation | async-start | bytes 3145728 | tf_op jit(solution)/shard_map/psum | solution.py:33
  71.6 181.6 %all-reduce.9.cloned.1.call-start = ((), (), s32[]{:S(2)}) async-start(), calls=%async_computation.1 | async-start | bytes 1572864 | tf_op jit(solution)/shard_map/psum | solution.py:68
  83.0 19.1 %copy-start.5 = (f32[2,2048]{1,0:T(2,128)S(1)}, f32[2,2048]{1,0:T(2,128)}, u32[]{:S(2)}) copy-start(f32[2,2048]{1,0:T(2,128)} %param.14) | copy-start | bytes 49156
  102.1 5.4 %copy-start.2 = (f32[96,2,2048]{2,0,1:T(8,128)S(1)}, f32[96,2,2048]{2,0,1:T(8,128)}, u32[]{:S(2)}) copy-start(f32[96,2,2048]{2,0,1:T(8,128)} %all-reduce.7.cloned.1.call-done) | copy-start | bytes 4718596
  102.1 5.7 %slice-start.2 = ((s8[4718592]{0:T(1024)(128)(4,1)}), s8[4194304]{0:T(1024)(128)(4,1)S(1)}, s32[]{:S(2)}) async-start(s8[4718592]{0:T(1024)(128)(4,1)} %bitcast.48), calls=%async_computation.5 | async-start | bytes 8388608
  103.9 4.0 %slice-start.3 = ((s8[4718592]{0:T(1024)(128)(4,1)}), s8[524288]{0:T(1024)(128)(4,1)S(1)}, s32[]{:S(2)}) async-start(s8[4718592]{0:T(1024)(128)(4,1)} %bitcast.48), calls=%async_computation.6 | async-start | bytes 1048576
  103.9 4.6 %copy-start.4 = (bf16[2048,1152]{1,0:T(8,128)(2,1)S(1)}, bf16[2048,1152]{1,0:T(8,128)(2,1)}, u32[]{:S(2)}) copy-start(bf16[2048,1152]{1,0:T(8,128)(2,1)} %get-tuple-element.6) | copy-start | bytes 14155780
  108.5 58.1 %copy-start.6 = (u32[32]{0:T(128)S(1)}, u32[32]{0:T(128)}, u32[]{:S(2)}) copy-start(u32[32]{0:T(128)} %constant.26) | copy-start | bytes 388
  159.6 8.5 %collective-permute-start.1 = (bf16[8,2304]{1,0:T(8,128)(2,1)S(1)}, bf16[8,2304]{1,0:T(8,128)(2,1)S(1)}, u32[]{:S(2)}, u32[]{:S(2)}) collective-permute-start(bf16[8,2304]{1,0:T(8,128)(2,1)S(1)} %convert.22), channel_id=1, source_target_pairs={{0,2},{1,3},{2,4},{3,5},{4,6},{5,7},{6,8},{7,9},{8,10},{9,11},{10,... | collective-permute-start | bytes 110600
  160.9 7.2 %collective-permute-start.2 = (bf16[8,2304]{1,0:T(8,128)(2,1)S(1)}, bf16[8,2304]{1,0:T(8,128)(2,1)S(1)}, u32[]{:S(2)}, u32[]{:S(2)}) collective-permute-start(bf16[8,2304]{1,0:T(8,128)(2,1)S(1)} %convert.22), channel_id=1, source_target_pairs={{0,3},{1,4},{2,5},{3,6},{4,7},{5,8},{6,9},{7,10},{8,11},{9,12},{10... | collective-permute-start | bytes 110600
  162.2 5.9 %collective-permute-start = (bf16[8,2304]{1,0:T(8,128)(2,1)S(1)}, bf16[8,2304]{1,0:T(8,128)(2,1)S(1)}, u32[]{:S(2)}, u32[]{:S(2)}) collective-permute-start(bf16[8,2304]{1,0:T(8,128)(2,1)S(1)} %convert.22), channel_id=1, source_target_pairs={{0,1},{1,2},{2,3},{3,4},{4,5},{5,6},{6,7},{7,8},{8,9},{9,10},{10,1... | collective-permute-start | bytes 110600
  164.1 4.0 %collective-permute-start.3 = (bf16[6,2304]{1,0:T(8,128)(2,1)S(1)}, bf16[6,2304]{1,0:T(8,128)(2,1)S(1)}, u32[]{:S(2)}, u32[]{:S(2)}) collective-permute-start(bf16[6,2304]{1,0:T(8,128)(2,1)S(1)} %slice.36), channel_id=1, source_target_pairs={{0,4},{1,5},{2,6},{3,7},{4,8},{5,9},{6,10},{7,11},{8,12},{9,13},{1... | collective-permute-start | bytes 82952
  221.5 10.9 %slice-start = ((s8[4718592]{0:T(1024)(128)(4,1)}), s8[4194304]{0:T(1024)(128)(4,1)S(1)}, s32[]{:S(2)}) async-start(s8[4718592]{0:T(1024)(128)(4,1)} %bitcast.46), calls=%async_computation.3 | async-start | bytes 8388608
  221.5 10.9 %slice-start.4 = ((s8[4718592]{0:T(1024)(128)(4,1)}), s8[4194304]{0:T(1024)(128)(4,1)S(1)}, s32[]{:S(2)}) async-start(s8[4718592]{0:T(1024)(128)(4,1)} %bitcast.50), calls=%async_computation.7 | async-start | bytes 8388608
  227.3 5.1 %slice-start.1 = ((s8[4718592]{0:T(1024)(128)(4,1)}), s8[524288]{0:T(1024)(128)(4,1)S(1)}, s32[]{:S(2)}) async-start(s8[4718592]{0:T(1024)(128)(4,1)} %bitcast.46), calls=%async_computation.4 | async-start | bytes 1048576
  227.3 5.1 %slice-start.5 = ((s8[4718592]{0:T(1024)(128)(4,1)}), s8[524288]{0:T(1024)(128)(4,1)S(1)}, s32[]{:S(2)}) async-start(s8[4718592]{0:T(1024)(128)(4,1)} %bitcast.50), calls=%async_computation.8 | async-start | bytes 1048576
  253.2 10.5 %copy-start.1 = (bf16[2,576,1152]{2,1,0:T(8,128)(2,1)S(1)}, bf16[2,576,1152]{2,1,0:T(8,128)(2,1)}, u32[]{:S(2)}) copy-start(bf16[2,576,1152]{2,1,0:T(8,128)(2,1)} %param.12) | copy-start | bytes 7962628
Sparse Core Ops, SparseCore 0:
  63.6 14.4 all-reduce.10
  80.5 21.5 all-reduce.6
  236.7 14.8 all-reduce.8
where the time goes:
time: 271 us; the launch traced here: 270 us
  blocking collectives  140 us (52%)
  matrix products  53 us (20%)
  other arithmetic  24.3 us (9%)
  waiting for transfers between devices  17.8 us (7%)
  between operations  14.6 us (5%)
  local copies, waits for them, and re-layouts  13.5 us (5%)
  starting transfers between devices  6.99 us (3%)
    unnamed x1, blocking collectives  49 us
    all_gather x1, blocking collectives, body(): normed = lax.all_gather(normed_local, 'feat', axis=1, tiled=True)  44.8 us
    all_gather x1, blocking collectives, body(): errors = lax.all_gather(errors_local, 'feat', axis=0, tiled=True)  43.6 us
    psum x1, waiting for transfers between devices, body(): preact = lax.psum(preact_part, 'mp')  17.4 us
    convert_element_type x1, other arithmetic, body(): grad_decoder = (loss_scale * jnp.stack([outer_product(active_first, error...  16.6 us
    dot_general x3, matrix products, outer_product(): lax.dot_general(weights_side, errors_side, (((0,), (0,)), ((), ())), pref...  15.9 us
    squeeze x1, local copies, waits for them, and re-layouts, body(): decoder[0]  11.3 us
    dot_general x1, matrix products, body(): jnp.einsum('ltd,lfd->tlf', normed, encoder, preferred_element_type=jnp.fl...  8.01 us
  transfers between devices with their start and end apart: 7, of which 2 were waited for; matrix products, arithmetic and copies ran while one was open for 14% of the time, Pallas kernels for 0%

commit v1 on v0

--- a/solution.py
+++ b/solution.py
@@ -19,7 +19,16 @@
     squares = lax.psum(jnp.sum(values * values, axis=2), "mp")
     inverse_rms = lax.rsqrt(squares / D + 1e-06)
     normed_local = (values * inverse_rms[:, :, None] * norm_gain[:, None, :]).astype(jnp.bfloat16)
-    normed = lax.all_gather(normed_local, "feat", axis=1, tiled=True)
+    ways = lax.axis_size("feat")
+    up = [(d, (d + 1) % ways) for d in range(ways)]
+    down = [(d, (d - 1) % ways) for d in range(ways)]
+    earlier, later = ([normed_local], [normed_local])
+    for _ in range(ways // 2):
+        earlier.append(lax.ppermute(earlier[-1], "feat", up))
+    for _ in range((ways - 1) // 2):
+        later.append(lax.ppermute(later[-1], "feat", down))
+    line = jnp.concatenate([*earlier[::-1], *later[1:]], axis=1)
+    normed = jnp.roll(line, (lax.axis_index("feat") - ways // 2) * normed_local.shape[1], axis=1)
     tokens = normed.shape[1]
     local_rows = residual.shape[1]
     gate_part = jnp.einsum("ltd,ldh->lth", normed, gate_weight, preferred_element_type=jnp.float32)

time: 271 us -> 318 us (1.17)
  blocking collectives: 140 us -> 95.2 us
  starting transfers between devices: 6.99 us -> 48.1 us
  local copies, waits for them, and re-layouts: 13.5 us -> 43.7 us
  waiting for transfers between devices: 17.8 us -> 35.7 us
    all_gather x1 -> x0, blocking collectives: 44.8 us -> none  [body(): normed = lax.all_gather(normed_local, 'feat', axis=1, tiled=True)]
    ppermute x0 -> x15, starting transfers between devices: none -> 41.2 us  [the longest x7 38.3 us: body(): later.append(lax.ppermute(later[-1], 'feat', down))]
    concatenate x0 -> x1, local copies, waits for them, and re-layouts: none -> 27.4 us  [body(): jnp.roll(line, (lax.axis_index('feat') - ways // 2) * normed_local.shape[...]
    ppermute x0 -> x15, waiting for transfers between devices: none -> 17.9 us  [the longest x8 16 us: body(): earlier.append(lax.ppermute(earlier[-1], 'feat', up))]
  transfers between devices with their start and end apart: 7 -> 22, of which waited for: 2 -> 17; matrix products, arithmetic and copies ran while one was open for 14% -> 12% of each run, Pallas kernels for 0% -> 0%
where the time goes in v1:
time: 318 us; the launch traced here: 315 us
  blocking collectives  95.2 us (30%)
  matrix products  53.3 us (17%)
  starting transfers between devices  48.1 us (15%)
  local copies, waits for them, and re-layouts  43.7 us (14%)
  waiting for transfers between devices  35.7 us (11%)
  other arithmetic  24.3 us (8%)
  between operations  14.7 us (5%)
    unnamed x1, blocking collectives  49 us
    all_gather x1, blocking collectives, body(): errors = lax.all_gather(errors_local, 'feat', axis=0, tiled=True)  43.6 us
    ppermute x7, starting transfers between devices, body(): later.append(lax.ppermute(later[-1], 'feat', down))  38.3 us
    concatenate x1, local copies, waits for them, and re-layouts, body(): jnp.roll(line, (lax.axis_index('feat') - ways // 2) * normed_local.shape[...  27.4 us
    psum x1, waiting for transfers between devices, body(): preact = lax.psum(preact_part, 'mp')  17.3 us
    convert_element_type x1, other arithmetic, body(): grad_decoder = (loss_scale * jnp.stack([outer_product(active_first, error...  16.6 us
    ppermute x8, waiting for transfers between devices, body(): earlier.append(lax.ppermute(earlier[-1], 'feat', up))  16 us
    dot_general x3, matrix products, outer_product(): lax.dot_general(weights_side, errors_side, (((0,), (0,)), ((), ())), pref...  15.9 us
  transfers between devices with their start and end apart: 22, of which 17 were waited for; matrix products, arithmetic and copies ran while one was open for 12% of the time, Pallas kernels for 0%

profile of v1, /device:TPU:0, one launch (start us, length us, event | category | flops | bytes accessed | tf_op | source)
XLA Modules:
  0.0 315.0 jit_solution(17201262854208628063)
XLA Ops:
  14.5 4.5 %collective-permute-start.8 = (bf16[2,6,1152]{2,1,0:T(8,128)(2,1)S(1)}, bf16[2,6,1152]{2,1,0:T(8,128)(2,1)S(1)}, u32[]{:S(2)}, u32[]{:S(2)}) collective-permute-start(bf16[2,6,1152]{2,1,0:T(8,128)(2,1)S(1)} %fusion.40), channel_id=1, source_target_pairs={{0,15},{1,0},{2,1},{3,2},{4,3},{5,4},{6,5},{7,6},{8,7},{9,8},{10,9... | collective-permute-start | bytes 82952 | tf_op jit(solution)/shard_map/ppermute | solution.py:29
  21.1 5.6 %collective-permute-start.9 = (bf16[2,6,1152]{2,1,0:T(8,128)(2,1)S(1)}, bf16[2,6,1152]{2,1,0:T(8,128)(2,1)S(1)}, u32[]{:S(2)}, u32[]{:S(2)}) collective-permute-start(bf16[2,6,1152]{2,1,0:T(8,128)(2,1)S(1)} %collective-permute-done.8), channel_id=1, source_target_pairs={{0,15},{1,0},{2,1},{3,2},{4,3},{5,4},{6,5},{7,6},{8,7},{9,8},{10,9... | collective-permute-start | bytes 82952 | tf_op jit(solution)/shard_map/ppermute | solution.py:29
  28.6 5.6 %collective-permute-start.10 = (bf16[2,6,1152]{2,1,0:T(8,128)(2,1)S(1)}, bf16[2,6,1152]{2,1,0:T(8,128)(2,1)S(1)}, u32[]{:S(2)}, u32[]{:S(2)}) collective-permute-start(bf16[2,6,1152]{2,1,0:T(8,128)(2,1)S(1)} %collective-permute-done.9), channel_id=1, source_target_pairs={{0,15},{1,0},{2,1},{3,2},{4,3},{5,4},{6,5},{7,6},{8,7},{9,8},{10,9... | collective-permute-start | bytes 82952 | tf_op jit(solution)/shard_map/ppermute | solution.py:29
  36.2 5.6 %collective-permute-start.11 = (bf16[2,6,1152]{2,1,0:T(8,128)(2,1)S(1)}, bf16[2,6,1152]{2,1,0:T(8,128)(2,1)S(1)}, u32[]{:S(2)}, u32[]{:S(2)}) collective-permute-start(bf16[2,6,1152]{2,1,0:T(8,128)(2,1)S(1)} %collective-permute-done.10), channel_id=1, source_target_pairs={{0,15},{1,0},{2,1},{3,2},{4,3},{5,4},{6,5},{7,6},{8,7},{9,8},{10,9... | collective-permute-start | bytes 82952 | tf_op jit(solution)/shard_map/ppermute | solution.py:29
  43.8 5.6 %collective-permute-start.12 = (bf16[2,6,1152]{2,1,0:T(8,128)(2,1)S(1)}, bf16[2,6,1152]{2,1,0:T(8,128)(2,1)S(1)}, u32[]{:S(2)}, u32[]{:S(2)}) collective-permute-start(bf16[2,6,1152]{2,1,0:T(8,128)(2,1)S(1)} %collective-permute-done.11), channel_id=1, source_target_pairs={{0,15},{1,0},{2,1},{3,2},{4,3},{5,4},{6,5},{7,6},{8,7},{9,8},{10,9... | collective-permute-start | bytes 82952 | tf_op jit(solution)/shard_map/ppermute | solution.py:29
  51.3 5.6 %collective-permute-start.13 = (bf16[2,6,1152]{2,1,0:T(8,128)(2,1)S(1)}, bf16[2,6,1152]{2,1,0:T(8,128)(2,1)S(1)}, u32[]{:S(2)}, u32[]{:S(2)}) collective-permute-start(bf16[2,6,1152]{2,1,0:T(8,128)(2,1)S(1)} %collective-permute-done.12), channel_id=1, source_target_pairs={{0,15},{1,0},{2,1},{3,2},{4,3},{5,4},{6,5},{7,6},{8,7},{9,8},{10,9... | collective-permute-start | bytes 82952 | tf_op jit(solution)/shard_map/ppermute | solution.py:29
  59.1 5.7 %collective-permute-start.14 = (bf16[2,6,1152]{2,1,0:T(8,128)(2,1)S(1)}, bf16[2,6,1152]{2,1,0:T(8,128)(2,1)S(1)}, u32[]{:S(2)}, u32[]{:S(2)}) collective-permute-start(bf16[2,6,1152]{2,1,0:T(8,128)(2,1)S(1)} %collective-permute-done.13), channel_id=1, source_target_pairs={{0,15},{1,0},{2,1},{3,2},{4,3},{5,4},{6,5},{7,6},{8,7},{9,8},{10,9... | collective-permute-start | bytes 82952 | tf_op jit(solution)/shard_map/ppermute | solution.py:29
  67.3 6.4 %collective-permute-done.7 = bf16[2,6,1152]{2,1,0:T(8,128)(2,1)} collective-permute-done((bf16[2,6,1152]{2,1,0:T(8,128)(2,1)S(1)}, bf16[2,6,1152]{2,1,0:T(8,128)(2,1)}, u32[]{:S(2)}, u32[]{:S(2)}) %collective-permute-start.7) | collective-permute-done | bytes 27680 | tf_op jit(solution)/shard_map/ppermute | solution.py:27
  73.7 27.4 %concatenate.15 = bf16[2,192,1152]{2,1,0:T(8,128)(2,1)S(1)} concatenate(bf16[2,6,1152]{2,1,0:T(8,128)(2,1)} %collective-permute-done.7, bf16[2,6,1152]{2,1,0:T(8,128)(2,1)} %copy-done.19, bf16[2,6,1152]{2,1,0:T(8,128)(2,1)} %copy-done.17, bf16[2,6,1152]{2,1,0:T(8,128)(2,1)} %copy-done.15, bf16[2,6,1152]{2,1,0:T(8,128)(2,1)} %copy-done.13, bf16[2,6,1152]{2,1,0:T(8,128)(2,1)} %copy-done.11, ...), dimensions={1} | concatenate | bytes 1769472 | tf_op jit(solution)/shard_map/jit(_roll_dynamic)/concatenate | solution.py:31
  101.1 3.7 %convolution_convert_fusion.3 = bf16[2,96,576]{2,1,0:T(8,128)(2,1)} fusion(bf16[2,1152,576]{1,2,0:T(8,128)(2,1)} %param.10, bf16[2,192,1152]{2,1,0:T(8,128)(2,1)S(1)} %concatenate.15, s32[]{:T(128)S(6)} %select_n.18), kind=kOutput, calls=%fused_computation.27 | convolution fusion | flops 254914560 | bytes 3317764 | tf_op jit(solution)/shard_map/ltd,ldh->lth/dot_general | solution.py:34
  104.9 3.4 %convolution_convert_fusion.2 = bf16[2,96,576]{2,1,0:T(8,128)(2,1)} fusion(bf16[2,1152,576]{1,2,0:T(8,128)(2,1)} %param.11, bf16[2,192,1152]{2,1,0:T(8,128)(2,1)S(1)} %concatenate.15, s32[]{:T(128)S(6)} %select_n.18), kind=kOutput, calls=%fused_computation.26 | convolution fusion | flops 254914560 | bytes 3317764 | tf_op jit(solution)/shard_map/ltd,ldh->lth/dot_general | solution.py:35
  108.4 8.0 %convolution_bitcast_fusion.4 = f32[96,2,2048]{2,0,1:T(8,128)} fusion(bf16[2,2048,1152]{2,1,0:T(8,128)(2,1)} %param.13, bf16[2,192,1152]{2,1,0:T(8,128)(2,1)S(1)} %concatenate.15, s32[]{:T(128)S(6)} %select_n.18), kind=kOutput, calls=%fused_computation.18 | convolution fusion | flops 905969664 | bytes 11452420 | tf_op jit(solution)/shard_map/ltd,lfd->tlf/dot_general | solution.py:41
  116.5 11.3 %slice_bitcast_fusion.2 = (bf16[2048,1152]{1,0:T(8,128)(2,1)}, bf16[2048,1152]{1,0:T(8,128)(2,1)}, bf16[2048,1152]{1,0:T(8,128)(2,1)}) fusion(bf16[3,2048,1152]{2,1,0:T(8,128)(2,1)} %param.15), kind=kLoop, calls=%fused_computation.16 | loop fusion | bytes 28311552 | tf_op jit(solution)/shard_map/squeeze | solution.py:52
  129.6 17.3 %all-reduce.7.cloned.1.call-done = f32[96,2,2048]{2,0,1:T(8,128)} async-done(((f32[96,2,2048]{2,0,1:T(8,128)}), f32[96,2,2048]{2,0,1:T(8,128)}) %all-reduce.7.cloned.1.call-update) | async-done | bytes 1572880 | tf_op jit(solution)/shard_map/psum | solution.py:42
  148.7 3.7 %fusion.24 = f32[96,1152]{1,0:T(8,128)S(1)} fusion(bf16[96,2,2048]{2,0,1:T(8,128)(2,1)S(1)} %maximum_convert_fusion, bf16[3,2048,1152]{2,1,0:T(8,128)(2,1)} %param.15), kind=kOutput, calls=%fused_computation.43 | convolution fusion | flops 452984832 | bytes 5554176 | tf_op jit(solution)/shard_map/dot_general | solution.py:52
  155.4 49.0 %fusion = f32[8,2304]{1,0:T(8,128)S(1)} fusion(f32[96,2304]{1,0:T(8,128)S(1)} %maximum_subtract_fusion), kind=kCustom, calls=%all-reduce-scatter | all-reduce-scatter fusion | flops 294913 | bytes 958976
  213.5 43.6 %all-gather = bf16[16,6,2304]{2,1,0:T(8,128)(2,1)S(1)} all-gather(bf16[1,6,2304]{2,1,0:T(8,128)(2,1)S(1)} %fusion.41), channel_id=1, replica_groups=mesh['mp'=2,'feat'=16] {'feat'}, dimensions={0}, use_global_device_ids=true | all-gather | bytes 470016 | tf_op jit(solution)/shard_map/all_gather | solution.py:65
  257.3 3.9 %fusion.16 = bf16[96,1,2048]{2,0,1:T(8,128)(2,1)S(1)} fusion(bf16[96,2304]{1,0:T(8,128)(2,1)S(1)} %reshape.18, bf16[3,2048,1152]{2,1,0:T(8,128)(2,1)} %param.15), kind=kOutput, calls=%fused_computation.22 | convolution fusion | flops 453181440 | bytes 5332992 | tf_op jit(solution)/shard_map/dot_general | solution.py:72
  261.2 5.1 %convolution_bitcast_fusion.1 = f32[1,2048,1152]{2,1,0:T(8,128)} fusion(bf16[96,2,2048]{2,0,1:T(8,128)(2,1)S(1)} %maximum_convert_fusion, bf16[96,2304]{1,0:T(8,128)(2,1)S(1)} %reshape.18), kind=kOutput, calls=%fused_computation.12 | convolution fusion | flops 452984832 | bytes 10051584 | tf_op jit(solution)/shard_map/dot_general | solution.py:12
  266.3 5.8 %convolution_bitcast_fusion = f32[1,2048,1152]{2,1,0:T(8,128)} fusion(bf16[96,2,2048]{2,0,1:T(8,128)(2,1)S(1)} %maximum_convert_fusion, bf16[96,2304]{1,0:T(8,128)(2,1)S(1)} %reshape.18), kind=kOutput, calls=%fused_computation.11 | convolution fusion | flops 452984832 | bytes 10051584 | tf_op jit(solution)/shard_map/dot_general | solution.py:12
  272.1 5.1 %convolution_bitcast_fusion.2 = f32[1,2048,1152]{2,1,0:T(8,128)} fusion(bf16[96,2,2048]{2,0,1:T(8,128)(2,1)S(1)} %maximum_convert_fusion, bf16[96,2304]{1,0:T(8,128)(2,1)S(1)} %reshape.18), kind=kOutput, calls=%fused_computation.13 | convolution fusion | flops 452984832 | bytes 10051584 | tf_op jit(solution)/shard_map/dot_general | solution.py:12
  277.2 3.1 fusion.13
  281.3 16.6 %fusion.1 = bf16[3,2048,1152]{2,1,0:T(8,128)(2,1)} fusion(f32[1,2048,1152]{2,1,0:T(8,128)} %convolution_bitcast_fusion, f32[1,2048,1152]{2,1,0:T(8,128)} %convolution_bitcast_fusion.1, f32[1,2048,1152]{2,1,0:T(8,128)} %convolution_bitcast_fusion.2), kind=kLoop, calls=%fused_computation.1 | loop fusion | flops 28311552 | bytes 42467328 | tf_op jit(solution)/shard_map/convert_element_type | solution.py:96
  300.8 7.7 %convolution_convert_fusion = bf16[2,2048,1152]{2,1,0:T(8,128)(2,1)} fusion(bf16[2,192,1152]{2,1,0:T(8,128)(2,1)} %copy-done.3, s32[]{:T(128)S(6)} %select_n.18, bf16[96,2,2048]{2,0,1:T(8,128)(2,1)} %all-reduce.9.cloned.1.call-done, bf16[96,2,2048]{2,0,1:T(8,128)(2,1)S(1)} %maximum_convert_fusion), kind=kOutput, calls=%fused_computation.2 | convolution fusion | flops 913047552 | bytes 11452420 | tf_op jit(solution)/shard_map/tlf,ltd->lfd/dot_general | solution.py:81
  (116 shorter events, 40.9 us)
Async XLA Ops:
  7.2 120.6 %copy-start = (bf16[2,576,1152]{2,1,0:T(8,128)(2,1)S(1)}, bf16[2,576,1152]{2,1,0:T(8,128)(2,1)}, u32[]{:S(2)}) copy-start(bf16[2,576,1152]{2,1,0:T(8,128)(2,1)} %param.12) | copy-start | bytes 7962628
  7.2 120.6 %all-reduce.11.cloned.1.call-start = ((), (), s32[]{:S(2)}) async-start(), calls=%async_computation.2 | async-start | bytes 983040 | tf_op jit(solution)/shard_map/psum | solution.py:37
  11.7 8.8 %collective-permute-start = (bf16[2,6,1152]{2,1,0:T(8,128)(2,1)S(1)}, bf16[2,6,1152]{2,1,0:T(8,128)(2,1)S(1)}, u32[]{:S(2)}, u32[]{:S(2)}) collective-permute-start(bf16[2,6,1152]{2,1,0:T(8,128)(2,1)S(1)} %fusion.40), channel_id=1, source_target_pairs={{0,1},{1,2},{2,3},{3,4},{4,5},{5,6},{6,7},{7,8},{8,9},{9,10},{10,1... | collective-permute-start | bytes 82952 | tf_op jit(solution)/shard_map/ppermute | solution.py:27
  14.5 6.2 %collective-permute-start.8 = (bf16[2,6,1152]{2,1,0:T(8,128)(2,1)S(1)}, bf16[2,6,1152]{2,1,0:T(8,128)(2,1)S(1)}, u32[]{:S(2)}, u32[]{:S(2)}) collective-permute-start(bf16[2,6,1152]{2,1,0:T(8,128)(2,1)S(1)} %fusion.40), channel_id=1, source_target_pairs={{0,15},{1,0},{2,1},{3,2},{4,3},{5,4},{6,5},{7,6},{8,7},{9,8},{10,9... | collective-permute-start | bytes 82952 | tf_op jit(solution)/shard_map/ppermute | solution.py:29
  20.5 7.6 %collective-permute-start.1 = (bf16[2,6,1152]{2,1,0:T(8,128)(2,1)S(1)}, bf16[2,6,1152]{2,1,0:T(8,128)(2,1)S(1)}, u32[]{:S(2)}, u32[]{:S(2)}) collective-permute-start(bf16[2,6,1152]{2,1,0:T(8,128)(2,1)S(1)} %collective-permute-done), channel_id=1, source_target_pairs={{0,1},{1,2},{2,3},{3,4},{4,5},{5,6},{6,7},{7,8},{8,9},{9,10},{10,1... | collective-permute-start | bytes 82952 | tf_op jit(solution)/shard_map/ppermute | solution.py:27
  21.1 7.2 %collective-permute-start.9 = (bf16[2,6,1152]{2,1,0:T(8,128)(2,1)S(1)}, bf16[2,6,1152]{2,1,0:T(8,128)(2,1)S(1)}, u32[]{:S(2)}, u32[]{:S(2)}) collective-permute-start(bf16[2,6,1152]{2,1,0:T(8,128)(2,1)S(1)} %collective-permute-done.8), channel_id=1, source_target_pairs={{0,15},{1,0},{2,1},{3,2},{4,3},{5,4},{6,5},{7,6},{8,7},{9,8},{10,9... | collective-permute-start | bytes 82952 | tf_op jit(solution)/shard_map/ppermute | solution.py:29
  28.0 7.6 %collective-permute-start.2 = (bf16[2,6,1152]{2,1,0:T(8,128)(2,1)S(1)}, bf16[2,6,1152]{2,1,0:T(8,128)(2,1)S(1)}, u32[]{:S(2)}, u32[]{:S(2)}) collective-permute-start(bf16[2,6,1152]{2,1,0:T(8,128)(2,1)S(1)} %collective-permute-done.1), channel_id=1, source_target_pairs={{0,1},{1,2},{2,3},{3,4},{4,5},{5,6},{6,7},{7,8},{8,9},{9,10},{10,1... | collective-permute-start | bytes 82952 | tf_op jit(solution)/shard_map/ppermute | solution.py:27
  28.6 7.3 %collective-permute-start.10 = (bf16[2,6,1152]{2,1,0:T(8,128)(2,1)S(1)}, bf16[2,6,1152]{2,1,0:T(8,128)(2,1)S(1)}, u32[]{:S(2)}, u32[]{:S(2)}) collective-permute-start(bf16[2,6,1152]{2,1,0:T(8,128)(2,1)S(1)} %collective-permute-done.9), channel_id=1, source_target_pairs={{0,15},{1,0},{2,1},{3,2},{4,3},{5,4},{6,5},{7,6},{8,7},{9,8},{10,9... | collective-permute-start | bytes 82952 | tf_op jit(solution)/shard_map/ppermute | solution.py:29
  35.6 7.6 %collective-permute-start.3 = (bf16[2,6,1152]{2,1,0:T(8,128)(2,1)S(1)}, bf16[2,6,1152]{2,1,0:T(8,128)(2,1)S(1)}, u32[]{:S(2)}, u32[]{:S(2)}) collective-permute-start(bf16[2,6,1152]{2,1,0:T(8,128)(2,1)S(1)} %collective-permute-done.2), channel_id=1, source_target_pairs={{0,1},{1,2},{2,3},{3,4},{4,5},{5,6},{6,7},{7,8},{8,9},{9,10},{10,1... | collective-permute-start | bytes 82952 | tf_op jit(solution)/shard_map/ppermute | solution.py:27
  36.2 7.3 %collective-permute-start.11 = (bf16[2,6,1152]{2,1,0:T(8,128)(2,1)S(1)}, bf16[2,6,1152]{2,1,0:T(8,128)(2,1)S(1)}, u32[]{:S(2)}, u32[]{:S(2)}) collective-permute-start(bf16[2,6,1152]{2,1,0:T(8,128)(2,1)S(1)} %collective-permute-done.10), channel_id=1, source_target_pairs={{0,15},{1,0},{2,1},{3,2},{4,3},{5,4},{6,5},{7,6},{8,7},{9,8},{10,9... | collective-permute-start | bytes 82952 | tf_op jit(solution)/shard_map/ppermute | solution.py:29
  43.1 7.6 %collective-permute-start.4 = (bf16[2,6,1152]{2,1,0:T(8,128)(2,1)S(1)}, bf16[2,6,1152]{2,1,0:T(8,128)(2,1)S(1)}, u32[]{:S(2)}, u32[]{:S(2)}) collective-permute-start(bf16[2,6,1152]{2,1,0:T(8,128)(2,1)S(1)} %collective-permute-done.3), channel_id=1, source_target_pairs={{0,1},{1,2},{2,3},{3,4},{4,5},{5,6},{6,7},{7,8},{8,9},{9,10},{10,1... | collective-permute-start | bytes 82952 | tf_op jit(solution)/shard_map/ppermute | solution.py:27
  43.8 7.3 %collective-permute-start.12 = (bf16[2,6,1152]{2,1,0:T(8,128)(2,1)S(1)}, bf16[2,6,1152]{2,1,0:T(8,128)(2,1)S(1)}, u32[]{:S(2)}, u32[]{:S(2)}) collective-permute-start(bf16[2,6,1152]{2,1,0:T(8,128)(2,1)S(1)} %collective-permute-done.11), channel_id=1, source_target_pairs={{0,15},{1,0},{2,1},{3,2},{4,3},{5,4},{6,5},{7,6},{8,7},{9,8},{10,9... | collective-permute-start | bytes 82952 | tf_op jit(solution)/shard_map/ppermute | solution.py:29
  50.7 7.8 %collective-permute-start.5 = (bf16[2,6,1152]{2,1,0:T(8,128)(2,1)S(1)}, bf16[2,6,1152]{2,1,0:T(8,128)(2,1)S(1)}, u32[]{:S(2)}, u32[]{:S(2)}) collective-permute-start(bf16[2,6,1152]{2,1,0:T(8,128)(2,1)S(1)} %collective-permute-done.4), channel_id=1, source_target_pairs={{0,1},{1,2},{2,3},{3,4},{4,5},{5,6},{6,7},{7,8},{8,9},{9,10},{10,1... | collective-permute-start | bytes 82952 | tf_op jit(solution)/shard_map/ppermute | solution.py:27
  51.3 7.4 %collective-permute-start.13 = (bf16[2,6,1152]{2,1,0:T(8,128)(2,1)S(1)}, bf16[2,6,1152]{2,1,0:T(8,128)(2,1)S(1)}, u32[]{:S(2)}, u32[]{:S(2)}) collective-permute-start(bf16[2,6,1152]{2,1,0:T(8,128)(2,1)S(1)} %collective-permute-done.12), channel_id=1, source_target_pairs={{0,15},{1,0},{2,1},{3,2},{4,3},{5,4},{6,5},{7,6},{8,7},{9,8},{10,9... | collective-permute-start | bytes 82952 | tf_op jit(solution)/shard_map/ppermute | solution.py:29
  58.5 7.6 %collective-permute-start.6 = (bf16[2,6,1152]{2,1,0:T(8,128)(2,1)S(1)}, bf16[2,6,1152]{2,1,0:T(8,128)(2,1)S(1)}, u32[]{:S(2)}, u32[]{:S(2)}) collective-permute-start(bf16[2,6,1152]{2,1,0:T(8,128)(2,1)S(1)} %collective-permute-done.5), channel_id=1, source_target_pairs={{0,1},{1,2},{2,3},{3,4},{4,5},{5,6},{6,7},{7,8},{8,9},{9,10},{10,1... | collective-permute-start | bytes 82952 | tf_op jit(solution)/shard_map/ppermute | solution.py:27
  59.1 7.3 %collective-permute-start.14 = (bf16[2,6,1152]{2,1,0:T(8,128)(2,1)S(1)}, bf16[2,6,1152]{2,1,0:T(8,128)(2,1)S(1)}, u32[]{:S(2)}, u32[]{:S(2)}) collective-permute-start(bf16[2,6,1152]{2,1,0:T(8,128)(2,1)S(1)} %collective-permute-done.13), channel_id=1, source_target_pairs={{0,15},{1,0},{2,1},{3,2},{4,3},{5,4},{6,5},{7,6},{8,7},{9,8},{10,9... | collective-permute-start | bytes 82952 | tf_op jit(solution)/shard_map/ppermute | solution.py:29
  66.1 7.7 %collective-permute-start.7 = (bf16[2,6,1152]{2,1,0:T(8,128)(2,1)S(1)}, bf16[2,6,1152]{2,1,0:T(8,128)(2,1)}, u32[]{:S(2)}, u32[]{:S(2)}) collective-permute-start(bf16[2,6,1152]{2,1,0:T(8,128)(2,1)S(1)} %collective-permute-done.6), channel_id=1, source_target_pairs={{0,1},{1,2},{2,3},{3,4},{4,5},{5,6},{6,7},{7,8},{8,9},{9,10},{10,1... | collective-permute-start | bytes 82952 | tf_op jit(solution)/shard_map/ppermute | solution.py:27
  108.3 38.6 %all-reduce.7.cloned.1.call-start = ((), (), s32[]{:S(2)}) async-start(), calls=%async_computation | async-start | bytes 3145728 | tf_op jit(solution)/shard_map/psum | solution.py:42
  116.4 181.5 %all-reduce.9.cloned.1.call-start = ((), (), s32[]{:S(2)}) async-start(), calls=%async_computation.1 | async-start | bytes 1572864 | tf_op jit(solution)/shard_map/psum | solution.py:77
  153.2 58.1 %copy-start.21 = (u32[32]{0:T(128)S(1)}, u32[32]{0:T(128)}, u32[]{:S(2)}) copy-start(u32[32]{0:T(128)} %constant.54) | copy-start | bytes 388
  204.4 8.5 %collective-permute-start.16 = (bf16[8,2304]{1,0:T(8,128)(2,1)S(1)}, bf16[8,2304]{1,0:T(8,128)(2,1)S(1)}, u32[]{:S(2)}, u32[]{:S(2)}) collective-permute-start(bf16[8,2304]{1,0:T(8,128)(2,1)S(1)} %convert.22), channel_id=1, source_target_pairs={{0,2},{1,3},{2,4},{3,5},{4,6},{5,7},{6,8},{7,9},{8,10},{9,11},{10,... | collective-permute-start | bytes 110600
  205.7 7.2 %collective-permute-start.17 = (bf16[8,2304]{1,0:T(8,128)(2,1)S(1)}, bf16[8,2304]{1,0:T(8,128)(2,1)S(1)}, u32[]{:S(2)}, u32[]{:S(2)}) collective-permute-start(bf16[8,2304]{1,0:T(8,128)(2,1)S(1)} %convert.22), channel_id=1, source_target_pairs={{0,3},{1,4},{2,5},{3,6},{4,7},{5,8},{6,9},{7,10},{8,11},{9,12},{10... | collective-permute-start | bytes 110600
  207.0 5.9 %collective-permute-start.15 = (bf16[8,2304]{1,0:T(8,128)(2,1)S(1)}, bf16[8,2304]{1,0:T(8,128)(2,1)S(1)}, u32[]{:S(2)}, u32[]{:S(2)}) collective-permute-start(bf16[8,2304]{1,0:T(8,128)(2,1)S(1)} %convert.22), channel_id=1, source_target_pairs={{0,1},{1,2},{2,3},{3,4},{4,5},{5,6},{6,7},{7,8},{8,9},{9,10},{10,1... | collective-permute-start | bytes 110600
  208.9 4.0 %collective-permute-start.18 = (bf16[6,2304]{1,0:T(8,128)(2,1)S(1)}, bf16[6,2304]{1,0:T(8,128)(2,1)S(1)}, u32[]{:S(2)}, u32[]{:S(2)}) collective-permute-start(bf16[6,2304]{1,0:T(8,128)(2,1)S(1)} %slice.36), channel_id=1, source_target_pairs={{0,4},{1,5},{2,6},{3,7},{4,8},{5,9},{6,10},{7,11},{8,12},{9,13},{1... | collective-permute-start | bytes 82952
  (26 other events, 146.6 us)
Sparse Core Ops, SparseCore 0:
  108.4 14.4 all-reduce.10
  125.3 21.5 all-reduce.6
  281.4 14.8 all-reduce.8
